TPU v7x, 32 devices: a whole 2x2x4 slice. The times are simulated.
32 devices in a mesh: py: 4 (over y, x), pz: 8 (over z, core).
Axes of the slice: x: 2, y: 2, z: 4, core: 2. Of those that a mesh axis runs over, the one named last changes fastest.
Arguments:
- field_one: float32 [256, 256, 512], P('py', 'pz'), may hold values from -6 to 6
- field_two: float32 [256, 256, 512], P('py', 'pz'), may hold values from -6 to 6
- coef: float32 [2, 2, 8], replicated, may hold values from -4 to 4
Outputs:
- potential_one: float32 [256, 256, 512], P('py', 'pz')
- potential_two: float32 [256, 256, 512], P('py', 'pz')
All inputs are finite; a program needn't handle non-finite values.
Results may differ from a plain program's by a relative error of at most 0.00013.
Values sent between devices are 32-bit elements; how exact they have to be, the bound alone decides.
No kernel may reach another device: no remote copies, remote signals or barrier semaphores. Data moves between devices by JAX's collectives and lax.ppermute only.
A program may use at most 256 MiB of HBM per device.

v0:
```python
import math
import jax
import jax.numpy as jnp
from jax import lax
from jax.sharding import PartitionSpec as P

HIGH = lax.Precision.HIGHEST


def padded_2(value, sides, width):
    for axis, dim in sides:
        size, length = (lax.axis_size(axis), value.shape[dim])
        up = [(i, (i + 1) % size) for i in range(size)]
        down = [(j, i) for i, j in up]
        last = lax.slice_in_dim(value, length - width, length, axis=dim)
        leading = lax.slice_in_dim(value, 0, width, axis=dim)
        before = lax.ppermute(last, axis, up)
        after = lax.ppermute(leading, axis, down)
        value = jnp.concatenate([before, value, after], axis=dim)
    return value


def freq_at(position, length):
    paired = position // 2
    odd_bit = position % 2
    inner = jnp.where(odd_bit == 0, paired, length - paired)
    return jnp.where(paired == 0, odd_bit * (length // 2), inner)


def scaled_signed(freq, length):
    return jnp.where(freq > length // 2, freq - length, freq).astype(jnp.float32) / length


def forward_table(length):
    indices = jnp.arange(length, dtype=jnp.int32)
    freq = freq_at(indices, length)
    phase = indices[:, None] * freq[None, :] % length
    angle = 2.0 * math.pi / length * phase.astype(jnp.float32)
    return (jnp.cos(angle), jnp.sin(angle))


def inverse_table(length):
    cosine, sine = forward_table(length)
    return (cosine.T / length, sine.T / length)


def contract(form, data, table):
    return jnp.einsum(form, data, table, precision=HIGH)


def complex_apply(form, real_part, imag_part, cosine, sine, sign):
    if imag_part is None:
        return (contract(form, real_part, cosine), -sign * contract(form, real_part, sine))
    real_out = contract(form, real_part, cosine) + sign * contract(form, imag_part, sine)
    imag_out = contract(form, imag_part, cosine) - sign * contract(form, real_part, sine)
    return (real_out, imag_out)


def make_kernel(coef, freqs, lengths):
    radius = scaled_signed(freqs[0], lengths[0]) ** 2 + scaled_signed(freqs[1], lengths[1]) ** 2
    radius = radius + scaled_signed(freqs[2], lengths[2]) ** 2
    ratio = 4.0 * radius / 3.0
    volume = ratio * jnp.sqrt(ratio)
    basis_count = coef.shape[2]
    centres = (jnp.arange(basis_count, dtype=jnp.float32) + 0.5) / basis_count
    basis = jnp.exp(-jnp.square((volume[None] - centres[:, None, None, None]) * basis_count))
    kernel = jnp.einsum("abr,rkxm->abkxm", coef, basis, precision=HIGH)
    return kernel


def shards(field_one, field_two, coef):
    y_local, z_local, x_count = field_one.shape
    py_count = lax.axis_size("py")
    pz_count = lax.axis_size("pz")
    y_count = y_local * py_count
    z_count = z_local * pz_count
    x_block = x_count // py_count
    ky_block = y_count // pz_count
    cells = y_local * z_local
    fields = jnp.stack([field_one, field_two])
    along_x = (4.0 * fields + jnp.roll(fields, 1, 3) + jnp.roll(fields, -1, 3)) / 6.0
    padded = padded_2(along_x, (("py", 1), ("pz", 2)), 1)
    along_y = (4.0 * padded[:, 1:-1] + padded[:, 2:] + padded[:, :-2]) / 6.0
    smoothed = (4.0 * along_y[:, :, 1:-1] + along_y[:, :, 2:] + along_y[:, :, :-2]) / 6.0
    flat = smoothed.reshape(2, cells, x_count)
    x_cos, x_sin = forward_table(x_count)
    real_part, imag_part = complex_apply("bsx,xq->bqs", flat, None, x_cos, x_sin, 1.0)
    batch = real_part.shape[0]
    y_cos, y_sin = forward_table(y_count)
    z_cos, z_sin = forward_table(z_count)
    zi_cos, zi_sin = inverse_table(z_count)
    yi_cos, yi_sin = inverse_table(y_count)
    xi_cos, xi_sin = inverse_table(x_count)
    real_in = lax.all_to_all(real_part, "py", split_axis=1, concat_axis=2, tiled=True)
    imag_in = lax.all_to_all(imag_part, "py", split_axis=1, concat_axis=2, tiled=True)
    items = real_in.shape[0]

    def relay(values):
        values = values.reshape(items, x_block, y_count, z_local).transpose(0, 2, 1, 3)
        return values.reshape(items, y_count, x_block * z_local)

    real_part, imag_part = complex_apply(
        "byc,yk->bkc", relay(real_in), relay(imag_in), y_cos, y_sin, 1.0
    )
    real_in = lax.all_to_all(real_part, "pz", split_axis=1, concat_axis=2, tiled=True)
    imag_in = lax.all_to_all(imag_part, "pz", split_axis=1, concat_axis=2, tiled=True)
    lines_items = real_in.shape[0]

    def relay(values):
        values = values.reshape(lines_items, ky_block, pz_count, x_block, z_local).transpose(
            0, 1, 3, 2, 4
        )
        return values.reshape(lines_items, ky_block, x_block, z_count)

    real_part, imag_part = complex_apply(
        "bkxz,zm->bkxm", relay(real_in), relay(imag_in), z_cos, z_sin, 1.0
    )
    ky_start = lax.axis_index("pz") * ky_block
    kx_start = lax.axis_index("py") * x_block
    freq_y = freq_at(ky_start + jnp.arange(ky_block, dtype=jnp.int32), y_count)
    freq_x = freq_at(kx_start + jnp.arange(x_block, dtype=jnp.int32), x_count)
    freq_z = freq_at(jnp.arange(z_count, dtype=jnp.int32), z_count)
    kernel = make_kernel(
        coef,
        (freq_y[:, None, None], freq_x[None, :, None], freq_z[None, None, :]),
        (y_count, x_count, z_count),
    )
    real_next = kernel[:, 0] * real_part[0] + kernel[:, 1] * real_part[1]
    imag_next = kernel[:, 0] * imag_part[0] + kernel[:, 1] * imag_part[1]
    real_part = real_next
    imag_part = imag_next
    real_part, imag_part = complex_apply(
        "bkxm,mz->bkxz", real_part, imag_part, zi_cos, zi_sin, -1.0
    )

    def relay_back(values):
        values = values.reshape(batch, ky_block, x_block, pz_count, z_local).transpose(
            0, 1, 3, 2, 4
        )
        return values.reshape(batch, ky_block, pz_count * x_block * z_local)

    real_part = relay_back(real_part)
    imag_part = relay_back(imag_part)
    real_in = lax.all_to_all(real_part, "pz", split_axis=2, concat_axis=1, tiled=True)
    imag_in = lax.all_to_all(imag_part, "pz", split_axis=2, concat_axis=1, tiled=True)
    back_items = real_in.shape[0]
    real_out, imag_out = complex_apply("bkc,ky->byc", real_in, imag_in, yi_cos, yi_sin, -1.0)

    def relay(values):
        values = values.reshape(back_items, y_count, x_block, z_local).transpose(0, 2, 1, 3)
        return values.reshape(back_items, x_block, y_count * z_local)

    real_part = relay(real_out)
    imag_part = relay(imag_out)
    real_in = lax.all_to_all(real_part, "py", split_axis=2, concat_axis=1, tiled=True)
    imag_in = lax.all_to_all(imag_part, "py", split_axis=2, concat_axis=1, tiled=True)
    result = contract("bqs,qx->bsx", real_in, xi_cos) - contract("bqs,qx->bsx", imag_in, xi_sin)
    return (
        result[0].reshape(y_local, z_local, x_count),
        result[1].reshape(y_local, z_local, x_count),
    )


def solution(mesh):
    in_specs = (P("py", "pz", None), P("py", "pz", None), P())
    out_specs = (P("py", "pz", None), P("py", "pz", None))
    return jax.shard_map(shards, mesh=mesh, in_specs=in_specs, out_specs=out_specs, check_vma=False)
```

profile of v0, /device:TPU:0, one launch (start us, length us, event | category | flops | bytes accessed | tf_op | source)
XLA Modules:
  0.0 1785.4 jit_solution(6525902035825200465)
XLA Ops:
  56.9 36.3 %convolution_bitcast_fusion = f32[2,512,2048]{2,1,0:T(8,128)S(1)} fusion(f32[2,2048,512]{2,1,0:T(8,128)} %bitcast.222, s32[512]{0:T(512)S(1)} %fusion.138), kind=kOutput, calls=%fused_computation.64 | convolution fusion | flops 12888571904 | bytes 16779264 | tf_op jit(solution)/shard_map/bsx,xq->bqs/dot_general | solution.py:48
  110.0 48.6 %multiply_bitcast_fusion = f32[2,512,2048]{2,1,0:T(8,128)S(1)} fusion(f32[2,2048,512]{2,1,0:T(8,128)} %bitcast.223, s32[512]{0:T(512)S(1)} %fusion.138), kind=kOutput, calls=%fused_computation.54 | convolution fusion | flops 12890669056 | bytes 16779264 | tf_op jit(solution)/shard_map/bsx,xq->bqs/dot_general | solution.py:48
  169.8 33.0 %all-to-all-done = f32[2,512,2048]{2,0,1:T(2,128)} async-done(((f32[2,512,2048]{2,0,1:T(2,128)}), f32[2,512,2048]{2,0,1:T(2,128)}, u32[]{:S(2)}, u32[]{:S(2)}) %all-to-all-start) | async-done | bytes 8388640 | tf_op jit(solution)/shard_map/all_to_all | solution.py:94
  239.1 62.9 %all-to-all-done.1 = f32[2,512,2048]{2,0,1:T(2,128)} async-done(((f32[2,512,2048]{2,0,1:T(2,128)}), f32[2,512,2048]{2,0,1:T(2,128)}, u32[]{:S(2)}, u32[]{:S(2)}) %all-to-all-start.1) | async-done | bytes 8388640 | tf_op jit(solution)/shard_map/all_to_all | solution.py:95
  406.5 150.7 %all-to-all-done.2 = f32[2,256,4096]{2,0,1:T(2,128)} async-done(((f32[2,256,4096]{2,0,1:T(2,128)}), f32[2,256,4096]{2,0,1:T(2,128)}, u32[]{:S(2)}, u32[]{:S(2)}) %all-to-all-start.2) | async-done | bytes 8388640 | tf_op jit(solution)/shard_map/all_to_all | solution.py:105
  564.1 58.6 %fusion.10 = f32[2,2,32,128,256]{4,1,0,3,2:T(2,128)} fusion(f32[8]{0:T(128)S(1)} %add_multiply_fusion, f32[32,128,256]{2,1,0:T(8,128)S(1)} %sqrt_multiply_fusion, f32[2,2,8]{2,1,0:T(2,128)S(1)} %copy-done), kind=kOutput, calls=%fused_computation.19 | convolution fusion | flops 436207616 | bytes 20971680 | tf_op jit(solution)/shard_map/abr,rkxm->abkxm/dot_general | solution.py:67
  674.5 21.7 %copy.133 = f32[2,32,128,8,32]{2,4,3,1,0:T(8,128)} copy(f32[2,32,128,8,32]{4,2,3,1,0:T(8,128)} %bitcast.202) | data formatting | bytes 16777216 | tf_op jit(solution)/shard_map/transpose | solution.py:110
  715.9 30.5 %all-to-all-done.3 = f32[2,256,4096]{2,0,1:T(2,128)} async-done(((f32[2,256,4096]{2,0,1:T(2,128)}), f32[2,256,4096]{2,0,1:T(2,128)}, u32[]{:S(2)}, u32[]{:S(2)}) %all-to-all-start.3) | async-done | bytes 8388640 | tf_op jit(solution)/shard_map/all_to_all | solution.py:106
  778.0 21.7 %copy.140 = f32[2,32,128,8,32]{2,4,3,1,0:T(8,128)} copy(f32[2,32,128,8,32]{4,2,3,1,0:T(8,128)} %bitcast.203) | data formatting | bytes 16777216 | tf_op jit(solution)/shard_map/transpose | solution.py:110
  866.1 30.2 %fusion.27 = (f32[2,32,128,256]{3,0,2,1:T(2,128)}, f32[2,32,128,256]{3,0,2,1:T(2,128)}) fusion(f32[2,1,32,128,256]{4,1,0,3,2:T(1,128)} %get-tuple-element.5, f32[2,1,32,128,256]{4,1,0,3,2:T(1,128)} %get-tuple-element.4, f32[32,128,256]{2,1,0:T(8,128)} %get-tuple-element.20, f32[32,128,256]{2,1,0:T(8,128)} %get-tuple-element.21, ...), kind=kLoop, calls=%fused_computation.44 | loop fusion | flops 12582912 | bytes 50331648 | tf_op jit(solution)/shard_map/add | solution.py:128
  929.7 28.6 %copy.203 = f32[2,32,8,128,32]{1,0,4,3,2:T(2,128)} copy(f32[2,32,8,128,32]{3,4,2,1,0:T(8,128)} %bitcast.233) | data formatting | bytes 16777216 | tf_op jit(solution)/shard_map/reshape | solution.py:140
  958.3 35.4 %reshape.323 = f32[8,1,262144]{2,1,0:T(1,128)} reshape(f32[32768,2,32]{2,1,0:T(2,128)} %bitcast.204) | data formatting | bytes 16777216
  1034.7 28.6 %copy.208 = f32[2,32,8,128,32]{1,0,4,3,2:T(2,128)} copy(f32[2,32,8,128,32]{3,4,2,1,0:T(8,128)} %bitcast.234) | data formatting | bytes 16777216 | tf_op jit(solution)/shard_map/reshape | solution.py:140
  1063.4 35.8 %reshape.321 = f32[8,1,262144]{2,1,0:T(1,128)} reshape(f32[32768,2,32]{2,1,0:T(2,128)} %bitcast.205) | data formatting | bytes 16777216
  1099.2 83.5 %all-to-all-done.4 = f32[8,1,262144]{2,1,0:T(1,128)} async-done(((f32[8,1,262144]{2,1,0:T(1,128)}), f32[8,1,262144]{2,1,0:T(1,128)}, u32[]{:S(2)}, u32[]{:S(2)}) %all-to-all-start.4) | async-done | bytes 8388640 | tf_op jit(solution)/shard_map/all_to_all | solution.py:144
  1188.2 28.2 %reduce.1 = f32[8,262144]{1,0:T(8,128)} reduce(f32[8,1,262144]{2,1,0:T(1,128)} %all-to-all-done.4, f32[]{:T(128)} %broadcast.767), dimensions={1}, to_apply=%all_to_all.108.reduce_sub_computation | reduce | bytes 16777220 | tf_op jit(solution)/shard_map/all_to_all | solution.py:144
  1216.4 55.1 %reshape.324 = f32[32768,2,32]{2,1,0:T(2,128)} reshape(f32[8,262144]{1,0:T(8,128)} %reduce.1) | data formatting | bytes 16777216
  1271.4 40.0 %copy.205 = f32[2,32,8,4096]{3,1,2,0:T(8,128)} copy(f32[2,32,8,4096]{1,0,3,2:T(2,128)} %bitcast.206) | data formatting | bytes 16777216 | tf_op jit(solution)/shard_map/all_to_all | solution.py:144
  1311.4 60.1 %all-to-all-done.5 = f32[8,1,262144]{2,1,0:T(1,128)} async-done(((f32[8,1,262144]{2,1,0:T(1,128)}), f32[8,1,262144]{2,1,0:T(1,128)}, u32[]{:S(2)}, u32[]{:S(2)}) %all-to-all-start.5) | async-done | bytes 8388640 | tf_op jit(solution)/shard_map/all_to_all | solution.py:145
  1371.5 28.2 %reduce = f32[8,262144]{1,0:T(8,128)} reduce(f32[8,1,262144]{2,1,0:T(1,128)} %all-to-all-done.5, f32[]{:T(128)} %broadcast.767), dimensions={1}, to_apply=%all_to_all.112.reduce_sub_computation | reduce | bytes 16777220 | tf_op jit(solution)/shard_map/all_to_all | solution.py:145
  1399.7 54.9 %reshape.322 = f32[32768,2,32]{2,1,0:T(2,128)} reshape(f32[8,262144]{1,0:T(8,128)} %reduce) | data formatting | bytes 16777216
  1454.6 40.0 %copy.210 = f32[2,32,8,4096]{3,1,2,0:T(8,128)} copy(f32[2,32,8,4096]{1,0,3,2:T(2,128)} %bitcast.207) | data formatting | bytes 16777216 | tf_op jit(solution)/shard_map/all_to_all | solution.py:145
  1623.6 30.8 %all-to-all-done.7 = f32[2,128,8192]{1,0,2:T(2,128)} async-done(((f32[2,128,8192]{1,0,2:T(2,128)}), f32[2,128,8192]{1,0,2:T(2,128)}, u32[]{:S(2)}, u32[]{:S(2)}) %all-to-all-start.7) | async-done | bytes 8388640 | tf_op jit(solution)/shard_map/all_to_all | solution.py:156
  1684.1 67.9 %all-to-all-done.6 = f32[2,128,8192]{1,0,2:T(2,128)} async-done(((f32[2,128,8192]{1,0,2:T(2,128)}), f32[2,128,8192]{1,0,2:T(2,128)}, u32[]{:S(2)}, u32[]{:S(2)}) %all-to-all-start.6) | async-done | bytes 8388640 | tf_op jit(solution)/shard_map/all_to_all | solution.py:155
  (105 shorter events, 672.7 us)
Async XLA Ops:
  0.6 563.5 %copy-start = (f32[2,2,8]{2,1,0:T(2,128)S(1)}, f32[2,2,8]{2,1,0:T(2,128)}, u32[]{:S(2)}) copy-start(f32[2,2,8]{2,1,0:T(2,128)} %param.5) | copy-start | bytes 388
  0.6 13.7 copy-start.5
  0.7 13.6 copy-start.6
  25.9 8.3 collective-permute-start
  29.0 7.5 collective-permute-start.1
  37.0 8.5 collective-permute-start.2
  37.1 8.5 collective-permute-start.3
  40.6 69.3 %copy-start.9 = (s32[512]{0:T(512)}, s32[512]{0:T(512)S(1)}, u32[]{:S(2)}) copy-start(s32[512]{0:T(512)S(1)} %fusion.138) | copy-start | bytes 6148
  104.3 98.5 %all-to-all-start = ((f32[2,512,2048]{2,0,1:T(2,128)}), f32[2,512,2048]{2,0,1:T(2,128)}, u32[]{:S(2)}, u32[]{:S(2)}) async-start(f32[2,512,2048]{2,0,1:T(2,128)} %copy.120), calls=%async_computation | async-start | bytes 16777216 | tf_op jit(solution)/shard_map/all_to_all | solution.py:94
  202.8 99.2 %all-to-all-start.1 = ((f32[2,512,2048]{2,0,1:T(2,128)}), f32[2,512,2048]{2,0,1:T(2,128)}, u32[]{:S(2)}, u32[]{:S(2)}) async-start(f32[2,512,2048]{2,0,1:T(2,128)} %copy.126), calls=%async_computation.1 | async-start | bytes 16777216 | tf_op jit(solution)/shard_map/all_to_all | solution.py:95
  332.7 13.9 copy-start.3
  368.1 189.0 %all-to-all-start.2 = ((f32[2,256,4096]{2,0,1:T(2,128)}), f32[2,256,4096]{2,0,1:T(2,128)}, u32[]{:S(2)}, u32[]{:S(2)}) async-start(f32[2,256,4096]{2,0,1:T(2,128)} %copy.131), calls=%async_computation.2 | async-start | bytes 16777216 | tf_op jit(solution)/shard_map/all_to_all | solution.py:105
  557.1 189.2 %all-to-all-start.3 = ((f32[2,256,4096]{2,0,1:T(2,128)}), f32[2,256,4096]{2,0,1:T(2,128)}, u32[]{:S(2)}, u32[]{:S(2)}) async-start(f32[2,256,4096]{2,0,1:T(2,128)} %copy.138), calls=%async_computation.3 | async-start | bytes 16777216 | tf_op jit(solution)/shard_map/all_to_all | solution.py:106
  799.7 19.4 %copy-start.2 = (f32[2,32,128,8,32]{2,4,3,1,0:T(8,128)S(1)}, f32[2,32,128,8,32]{2,4,3,1,0:T(8,128)}, u32[]{:S(2)}) copy-start(f32[2,32,128,8,32]{2,4,3,1,0:T(8,128)} %copy.140) | copy-start | bytes 25165828
  799.7 40.6 %slice-start = ((s8[8388608]{0:T(1024)(128)(4,1)}), s8[4194304]{0:T(1024)(128)(4,1)S(1)}, s32[]{:S(2)}) async-start(s8[8388608]{0:T(1024)(128)(4,1)} %bitcast.213), calls=%async_computation.8 | async-start | bytes 8388608
  819.1 21.2 %slice-start.1 = ((s8[8388608]{0:T(1024)(128)(4,1)}), s8[4194304]{0:T(1024)(128)(4,1)S(1)}, s32[]{:S(2)}) async-start(s8[8388608]{0:T(1024)(128)(4,1)} %bitcast.213), calls=%async_computation.9 | async-start | bytes 8388608
  840.3 18.4 %copy-start.8 = (f32[2,32,128,256]{3,2,1,0:T(8,128)S(1)}, f32[2,32,128,256]{3,2,1,0:T(8,128)}, u32[]{:S(2)}) copy-start(f32[2,32,128,256]{3,2,1,0:T(8,128)} %convolution_add_fusion) | copy-start | bytes 25165828
  896.4 13.0 copy-start.4
  993.7 189.0 %all-to-all-start.4 = ((f32[8,1,262144]{2,1,0:T(1,128)}), f32[8,1,262144]{2,1,0:T(1,128)}, u32[]{:S(2)}, u32[]{:S(2)}) async-start(f32[8,1,262144]{2,1,0:T(1,128)} %reshape.323), calls=%async_computation.4 | async-start | bytes 16777216 | tf_op jit(solution)/shard_map/all_to_all | solution.py:144
  1182.7 188.8 %all-to-all-start.5 = ((f32[8,1,262144]{2,1,0:T(1,128)}), f32[8,1,262144]{2,1,0:T(1,128)}, u32[]{:S(2)}, u32[]{:S(2)}) async-start(f32[8,1,262144]{2,1,0:T(1,128)} %reshape.321), calls=%async_computation.5 | async-start | bytes 16777216 | tf_op jit(solution)/shard_map/all_to_all | solution.py:145
  1556.3 98.2 %all-to-all-start.7 = ((f32[2,128,8192]{1,0,2:T(2,128)}), f32[2,128,8192]{1,0,2:T(2,128)}, u32[]{:S(2)}, u32[]{:S(2)}) async-start(f32[2,128,8192]{1,0,2:T(2,128)} %copy.172), calls=%async_computation.7 | async-start | bytes 16777216 | tf_op jit(solution)/shard_map/all_to_all | solution.py:156
  1654.4 97.6 %all-to-all-start.6 = ((f32[2,128,8192]{1,0,2:T(2,128)}), f32[2,128,8192]{1,0,2:T(2,128)}, u32[]{:S(2)}, u32[]{:S(2)}) async-start(f32[2,128,8192]{1,0,2:T(2,128)} %copy.167), calls=%async_computation.6 | async-start | bytes 16777216 | tf_op jit(solution)/shard_map/all_to_all | solution.py:155
  1752.0 7.7 copy-start.7
  1759.7 25.5 %copy-start.1 = (f32[2,2,8]{2,1,0:T(2,128)S(1)}, f32[2,2,8]{2,1,0:T(2,128)}, u32[]{:S(2)}) copy-start(f32[2,2,8]{2,1,0:T(2,128)} %param.5) | copy-start | bytes 388
  (1 other events, 3.9 us)
where the time goes:
time: 1800 us; the launch traced here: 1790 us
  local copies, waits for them, and re-layouts  661 us (37%)
  waiting for transfers between devices  531 us (30%)
  matrix products  416 us (23%)
  other arithmetic  125 us (7%)
  starting transfers between devices  51 us (3%)
    dot_general x20, matrix products, contract(): return jnp.einsum(form, data, table, precision=HIGH)  357 us
    unnamed x30, local copies, waits for them, and re-layouts  181 us
    all_to_all x1, waiting for transfers between devices, shards(): lax.all_to_all(real_part, 'pz', split_axis=1, concat_axis=2, tiled=True)  151 us
    all_to_all x1, waiting for transfers between devices, shards(): lax.all_to_all(real_part, 'pz', split_axis=2, concat_axis=1, tiled=True)  83.5 us
    all_to_all x1, waiting for transfers between devices, shards(): lax.all_to_all(real_part, 'py', split_axis=2, concat_axis=1, tiled=True)  67.9 us
    all_to_all x1, waiting for transfers between devices, shards(): lax.all_to_all(imag_part, 'py', split_axis=1, concat_axis=2, tiled=True)  62.9 us
    all_to_all x1, waiting for transfers between devices, shards(): lax.all_to_all(imag_part, 'pz', split_axis=2, concat_axis=1, tiled=True)  60.1 us
    dot_general x1, matrix products, make_kernel(): kernel = jnp.einsum('abr,rkxm->abkxm', coef, basis, precision=HIGH)  58.6 us
  transfers between devices with their start and end apart: 12, of which 11 were waited for; matrix products, arithmetic and copies ran while one was open for 33% of the time, Pallas kernels for 0%

commit v1 on v0

--- a/solution.py
+++ b/solution.py
@@ -1,10 +1,31 @@
+import functools
 import math
 import jax
 import jax.numpy as jnp
 from jax import lax
 from jax.sharding import PartitionSpec as P
+from jax.lax import axis_index, axis_size, ppermute
 
 HIGH = lax.Precision.HIGHEST
+
+
+def mark_threads(view, row_axis):
+    upper, raw_out = (axis_size(row_axis), axis_index(row_axis))
+    mid_arr = list(view.shape)
+    odd = view.shape[2] // upper
+    mid_arr[2] = odd
+    r1 = mid_arr[1]
+    mid_arr[1] = r1 * upper
+    work_now = jnp.zeros(mid_arr, view.dtype)
+    for b in range(upper):
+        n_now = lax.dynamic_slice_in_dim(view, (raw_out ^ b) * odd, odd, axis=2)
+        if b:
+            n_now = ppermute(n_now, row_axis, perm=[(idx, idx ^ b) for idx in range(upper)])
+        work_now = lax.dynamic_update_slice_in_dim(work_now, n_now, (raw_out ^ b) * r1, axis=1)
+    return work_now
+
+
+space_place = functools.partial(mark_threads, row_axis="pz")
 
 
 def padded_2(value, sides, width):
@@ -141,7 +162,7 @@
 
     real_part = relay_back(real_part)
     imag_part = relay_back(imag_part)
-    real_in = lax.all_to_all(real_part, "pz", split_axis=2, concat_axis=1, tiled=True)
+    real_in = space_place(real_part)
     imag_in = lax.all_to_all(imag_part, "pz", split_axis=2, concat_axis=1, tiled=True)
     back_items = real_in.shape[0]
     real_out, imag_out = complex_apply("bkc,ky->byc", real_in, imag_in, yi_cos, yi_sin, -1.0)

time: 1800 us -> 1790 us (level)
  the two profiles are of different devices: /device:TPU:0 before, /device:TPU:8 now
where the time goes in v1:
time: 1790 us; the launch traced here: 1780 us
  waiting for transfers between devices  641 us (36%)
  local copies, waits for them, and re-layouts  563 us (31%)
  matrix products  416 us (23%)
  other arithmetic  96.9 us (5%)
  starting transfers between devices  58 us (3%)
    dot_general x20, matrix products, contract(): return jnp.einsum(form, data, table, precision=HIGH)  357 us
    ppermute x7, waiting for transfers between devices, mark_threads(): ppermute(n_now, row_axis, perm=[(idx, idx ^ b) for idx in range(upper)])  258 us
    all_to_all x1, waiting for transfers between devices, shards(): lax.all_to_all(real_part, 'pz', split_axis=1, concat_axis=2, tiled=True)  147 us
    unnamed x30, local copies, waits for them, and re-layouts  91.5 us
    all_to_all x1, waiting for transfers between devices, shards(): lax.all_to_all(real_part, 'py', split_axis=2, concat_axis=1, tiled=True)  68.3 us
    all_to_all x1, waiting for transfers between devices, shards(): lax.all_to_all(imag_part, 'py', split_axis=1, concat_axis=2, tiled=True)  62.1 us
    dot_general x1, matrix products, make_kernel(): kernel = jnp.einsum('abr,rkxm->abkxm', coef, basis, precision=HIGH)  58.6 us
    reshape x2, local copies, waits for them, and re-layouts, relay_back(): return values.reshape(batch, ky_block, pz_count * x_block * z_local)  49.9 us
  transfers between devices with their start and end apart: 18, of which 16 were waited for; matrix products, arithmetic and copies ran while one was open for 26% of the time, Pallas kernels for 0%

profile of v1, /device:TPU:8, one launch (start us, length us, event | category | flops | bytes accessed | tf_op | source)
XLA Modules:
  0.0 1775.5 jit_solution(15262660960577489617)
XLA Ops:
  55.3 36.3 %convolution_bitcast_fusion = f32[2,512,2048]{2,1,0:T(8,128)S(1)} fusion(f32[2,2048,512]{2,1,0:T(8,128)} %bitcast.212, s32[512]{0:T(512)S(1)} %fusion.158), kind=kOutput, calls=%fused_computation.64 | convolution fusion | flops 12888571904 | bytes 16779264 | tf_op jit(solution)/shard_map/bsx,xq->bqs/dot_general | solution.py:69
  108.4 48.6 %multiply_bitcast_fusion = f32[2,512,2048]{2,1,0:T(8,128)S(1)} fusion(f32[2,2048,512]{2,1,0:T(8,128)} %bitcast.213, s32[512]{0:T(512)S(1)} %fusion.158), kind=kOutput, calls=%fused_computation.54 | convolution fusion | flops 12890669056 | bytes 16779264 | tf_op jit(solution)/shard_map/bsx,xq->bqs/dot_general | solution.py:69
  168.2 33.9 %all-to-all-done = f32[2,512,2048]{2,0,1:T(2,128)} async-done(((f32[2,512,2048]{2,0,1:T(2,128)}), f32[2,512,2048]{2,0,1:T(2,128)}, u32[]{:S(2)}, u32[]{:S(2)}) %all-to-all-start) | async-done | bytes 8388640 | tf_op jit(solution)/shard_map/all_to_all | solution.py:115
  238.3 62.1 %all-to-all-done.1 = f32[2,512,2048]{2,0,1:T(2,128)} async-done(((f32[2,512,2048]{2,0,1:T(2,128)}), f32[2,512,2048]{2,0,1:T(2,128)}, u32[]{:S(2)}, u32[]{:S(2)}) %all-to-all-start.1) | async-done | bytes 8388640 | tf_op jit(solution)/shard_map/all_to_all | solution.py:116
  405.3 147.2 %all-to-all-done.2 = f32[2,256,4096]{2,0,1:T(2,128)} async-done(((f32[2,256,4096]{2,0,1:T(2,128)}), f32[2,256,4096]{2,0,1:T(2,128)}, u32[]{:S(2)}, u32[]{:S(2)}) %all-to-all-start.2) | async-done | bytes 8388640 | tf_op jit(solution)/shard_map/all_to_all | solution.py:126
  562.9 58.6 %fusion.10 = f32[2,2,32,128,256]{4,1,0,3,2:T(2,128)} fusion(f32[8]{0:T(128)S(1)} %add_multiply_fusion, f32[32,128,256]{2,1,0:T(8,128)S(1)} %sqrt_multiply_fusion, f32[2,2,8]{2,1,0:T(2,128)S(1)} %copy-done), kind=kOutput, calls=%fused_computation.19 | convolution fusion | flops 436207616 | bytes 20971680 | tf_op jit(solution)/shard_map/abr,rkxm->abkxm/dot_general | solution.py:88
  673.4 21.7 %copy.130 = f32[2,32,128,8,32]{2,4,3,1,0:T(8,128)} copy(f32[2,32,128,8,32]{4,2,3,1,0:T(8,128)} %bitcast.196) | data formatting | bytes 16777216 | tf_op jit(solution)/shard_map/transpose | solution.py:131
  714.9 26.8 %all-to-all-done.3 = f32[2,256,4096]{2,0,1:T(2,128)} async-done(((f32[2,256,4096]{2,0,1:T(2,128)}), f32[2,256,4096]{2,0,1:T(2,128)}, u32[]{:S(2)}, u32[]{:S(2)}) %all-to-all-start.3) | async-done | bytes 8388640 | tf_op jit(solution)/shard_map/all_to_all | solution.py:127
  773.3 21.7 %copy.137 = f32[2,32,128,8,32]{2,4,3,1,0:T(8,128)} copy(f32[2,32,128,8,32]{4,2,3,1,0:T(8,128)} %bitcast.197) | data formatting | bytes 16777216 | tf_op jit(solution)/shard_map/transpose | solution.py:131
  814.5 21.1 %convolution_add_fusion = f32[2,32,128,256]{3,2,1,0:T(8,128)} fusion(f32[2,32,128,256]{3,2,1,0:T(8,128)} %fusion.91, f32[2,32,128,256]{2,3,1,0:T(8,128)S(1)} %bitcast.207, s32[256]{0:T(256)S(1)} %compare_select_fusion.8), kind=kOutput, calls=%fused_computation.71 | convolution fusion | flops 6445465600 | bytes 25166848 | tf_op jit(solution)/shard_map/bkxz,zm->bkxm/dot_general | solution.py:69
  861.5 30.3 %fusion.27 = (f32[2,32,128,256]{3,0,2,1:T(2,128)}, f32[2,32,128,256]{3,0,2,1:T(2,128)}) fusion(f32[2,1,32,128,256]{4,1,0,3,2:T(1,128)} %get-tuple-element.5, f32[2,1,32,128,256]{4,1,0,3,2:T(1,128)} %get-tuple-element.4, f32[32,128,256]{2,1,0:T(8,128)} %get-tuple-element.28, f32[32,128,256]{2,1,0:T(8,128)} %get-tuple-element.29, ...), kind=kLoop, calls=%fused_computation.44 | loop fusion | flops 12582912 | bytes 50331648 | tf_op jit(solution)/shard_map/add | solution.py:149
  924.6 28.7 %copy.199 = f32[2,32,8,128,32]{1,0,4,3,2:T(2,128)} copy(f32[2,32,8,128,32]{3,4,2,1,0:T(8,128)} %bitcast.223) | data formatting | bytes 16777216 | tf_op jit(solution)/shard_map/reshape | solution.py:161
  953.3 35.4 %reshape.321 = f32[8,1,262144]{2,1,0:T(1,128)} reshape(f32[32768,2,32]{2,1,0:T(2,128)} %bitcast.198) | data formatting | bytes 16777216
  1053.0 21.2 %reshape.296 = f32[2,32,32768]{2,1,0:T(8,128)} reshape(f32[2,32,8,128,32]{4,3,2,1,0:T(8,128)} %copy.149) | data formatting | bytes 16777216 | tf_op jit(solution)/shard_map/reshape | solution.py:161
  1091.7 64.9 %collective-permute-done.5 = f32[2,32,4096]{2,1,0:T(8,128)} collective-permute-done((f32[2,32,4096]{2,1,0:T(8,128)}, f32[2,32,4096]{2,1,0:T(8,128)}, u32[]{:S(2)}, u32[]{:S(2)}) %collective-permute-start.5) | collective-permute-done | bytes 1048608 | tf_op jit(solution)/shard_map/ppermute | solution.py:23
  1180.8 109.3 %collective-permute-done.7 = f32[2,32,4096]{2,1,0:T(8,128)S(1)} collective-permute-done((f32[2,32,4096]{2,1,0:T(8,128)}, f32[2,32,4096]{2,1,0:T(8,128)S(1)}, u32[]{:S(2)}, u32[]{:S(2)}) %collective-permute-start.7) | collective-permute-done | bytes 1048608 | tf_op jit(solution)/shard_map/ppermute | solution.py:23
  1291.2 21.3 %collective-permute-done.8 = f32[2,32,4096]{2,1,0:T(8,128)S(1)} collective-permute-done((f32[2,32,4096]{2,1,0:T(8,128)S(1)}, f32[2,32,4096]{2,1,0:T(8,128)S(1)}, u32[]{:S(2)}, u32[]{:S(2)}) %collective-permute-start.8) | collective-permute-done | bytes 1048608 | tf_op jit(solution)/shard_map/ppermute | solution.py:23
  1313.6 24.0 %collective-permute-done.9 = f32[2,32,4096]{2,1,0:T(8,128)S(1)} collective-permute-done((f32[2,32,4096]{2,1,0:T(8,128)S(1)}, f32[2,32,4096]{2,1,0:T(8,128)S(1)}, u32[]{:S(2)}, u32[]{:S(2)}) %collective-permute-start.9) | collective-permute-done | bytes 1048608 | tf_op jit(solution)/shard_map/ppermute | solution.py:23
  1360.5 28.2 %reduce = f32[8,262144]{1,0:T(8,128)} reduce(f32[8,1,262144]{2,1,0:T(1,128)} %all-to-all-done.4, f32[]{:T(128)} %broadcast.785), dimensions={1}, to_apply=%all_to_all.95.reduce_sub_computation | reduce | bytes 16777220 | tf_op jit(solution)/shard_map/all_to_all | solution.py:166
  1388.6 54.9 %reshape.322 = f32[32768,2,32]{2,1,0:T(2,128)} reshape(f32[8,262144]{1,0:T(8,128)} %reduce) | data formatting | bytes 16777216
  1443.5 40.0 %copy.201 = f32[2,32,8,4096]{3,1,2,0:T(8,128)} copy(f32[2,32,8,4096]{1,0,3,2:T(2,128)} %bitcast.199) | data formatting | bytes 16777216 | tf_op jit(solution)/shard_map/all_to_all | solution.py:166
  1612.5 31.7 %all-to-all-done.6 = f32[2,128,8192]{1,0,2:T(2,128)} async-done(((f32[2,128,8192]{1,0,2:T(2,128)}), f32[2,128,8192]{1,0,2:T(2,128)}, u32[]{:S(2)}, u32[]{:S(2)}) %all-to-all-start.6) | async-done | bytes 8388640 | tf_op jit(solution)/shard_map/all_to_all | solution.py:177
  1673.8 68.3 %all-to-all-done.5 = f32[2,128,8192]{1,0,2:T(2,128)} async-done(((f32[2,128,8192]{1,0,2:T(2,128)}), f32[2,128,8192]{1,0,2:T(2,128)}, u32[]{:S(2)}, u32[]{:S(2)}) %all-to-all-start.5) | async-done | bytes 8388640 | tf_op jit(solution)/shard_map/all_to_all | solution.py:176
  1749.8 21.1 %fusion.37 = f32[2,2048,512]{2,1,0:T(8,128)S(1)} fusion(f32[2,2048,512]{2,1,0:T(8,128)S(1)} %copy-done.8, f32[2,4,256,8,128]{4,3,2,1,0:T(8,128)} %bitcast.220, s32[512]{0:T(512)S(1)} %copy-done.11), kind=kOutput, calls=%fused_computation.69 | convolution fusion | flops 12890931200 | bytes 25167872 | tf_op jit(solution)/shard_map/bqs,qx->bsx/dot_general | solution.py:69
  (125 shorter events, 717.0 us)
Async XLA Ops:
  0.6 562.2 %copy-start = (f32[2,2,8]{2,1,0:T(2,128)S(1)}, f32[2,2,8]{2,1,0:T(2,128)}, u32[]{:S(2)}) copy-start(f32[2,2,8]{2,1,0:T(2,128)} %param.5) | copy-start | bytes 388
  25.8 7.3 collective-permute-start
  27.3 7.5 collective-permute-start.1
  35.4 6.3 collective-permute-start.2
  35.5 8.5 collective-permute-start.3
  37.2 71.2 %copy-start.10 = (s32[512]{0:T(512)}, s32[512]{0:T(512)S(1)}, u32[]{:S(2)}) copy-start(s32[512]{0:T(512)S(1)} %fusion.158) | copy-start | bytes 6148
  102.7 99.3 %all-to-all-start = ((f32[2,512,2048]{2,0,1:T(2,128)}), f32[2,512,2048]{2,0,1:T(2,128)}, u32[]{:S(2)}, u32[]{:S(2)}) async-start(f32[2,512,2048]{2,0,1:T(2,128)} %copy.117), calls=%async_computation | async-start | bytes 16777216 | tf_op jit(solution)/shard_map/all_to_all | solution.py:115
  202.0 98.4 %all-to-all-start.1 = ((f32[2,512,2048]{2,0,1:T(2,128)}), f32[2,512,2048]{2,0,1:T(2,128)}, u32[]{:S(2)}, u32[]{:S(2)}) async-start(f32[2,512,2048]{2,0,1:T(2,128)} %copy.123), calls=%async_computation.1 | async-start | bytes 16777216 | tf_op jit(solution)/shard_map/all_to_all | solution.py:116
  366.6 185.8 %all-to-all-start.2 = ((f32[2,256,4096]{2,0,1:T(2,128)}), f32[2,256,4096]{2,0,1:T(2,128)}, u32[]{:S(2)}, u32[]{:S(2)}) async-start(f32[2,256,4096]{2,0,1:T(2,128)} %copy.128), calls=%async_computation.2 | async-start | bytes 16777216 | tf_op jit(solution)/shard_map/all_to_all | solution.py:126
  552.4 189.2 %all-to-all-start.3 = ((f32[2,256,4096]{2,0,1:T(2,128)}), f32[2,256,4096]{2,0,1:T(2,128)}, u32[]{:S(2)}, u32[]{:S(2)}) async-start(f32[2,256,4096]{2,0,1:T(2,128)} %copy.135), calls=%async_computation.3 | async-start | bytes 16777216 | tf_op jit(solution)/shard_map/all_to_all | solution.py:127
  795.0 19.5 %copy-start.2 = (f32[2,32,128,8,32]{2,4,3,1,0:T(8,128)S(1)}, f32[2,32,128,8,32]{2,4,3,1,0:T(8,128)}, u32[]{:S(2)}) copy-start(f32[2,32,128,8,32]{2,4,3,1,0:T(8,128)} %copy.137) | copy-start | bytes 25165828
  795.0 40.7 %slice-start = ((s8[8388608]{0:T(1024)(128)(4,1)}), s8[4194304]{0:T(1024)(128)(4,1)S(1)}, s32[]{:S(2)}) async-start(s8[8388608]{0:T(1024)(128)(4,1)} %bitcast.201), calls=%async_computation.7 | async-start | bytes 8388608
  814.5 21.1 %slice-start.1 = ((s8[8388608]{0:T(1024)(128)(4,1)}), s8[4194304]{0:T(1024)(128)(4,1)S(1)}, s32[]{:S(2)}) async-start(s8[8388608]{0:T(1024)(128)(4,1)} %bitcast.201), calls=%async_computation.8 | async-start | bytes 8388608
  988.7 371.2 %all-to-all-start.4 = ((f32[8,1,262144]{2,1,0:T(1,128)}), f32[8,1,262144]{2,1,0:T(1,128)}, u32[]{:S(2)}, u32[]{:S(2)}) async-start(f32[8,1,262144]{2,1,0:T(1,128)} %reshape.321), calls=%async_computation.4 | async-start | bytes 16777216 | tf_op jit(solution)/shard_map/all_to_all | solution.py:166
  1083.3 4.6 collective-permute-start.4
  1083.5 73.0 %collective-permute-start.5 = (f32[2,32,4096]{2,1,0:T(8,128)}, f32[2,32,4096]{2,1,0:T(8,128)}, u32[]{:S(2)}, u32[]{:S(2)}) collective-permute-start(f32[2,32,4096]{2,1,0:T(8,128)} %get-tuple-element.15), channel_id=1, source_target_pairs={{0,2},{1,3},{2,0},{3,1},{4,6},{5,7},{6,4},{7,5},{8,10},{9,11},{10,... | collective-permute-start | bytes 3145736 | tf_op jit(solution)/shard_map/ppermute | solution.py:23
  1083.9 94.7 %collective-permute-start.6 = (f32[2,32,4096]{2,1,0:T(8,128)}, f32[2,32,4096]{2,1,0:T(8,128)}, u32[]{:S(2)}, u32[]{:S(2)}) collective-permute-start(f32[2,32,4096]{2,1,0:T(8,128)} %get-tuple-element.14), channel_id=1, source_target_pairs={{0,3},{1,2},{2,1},{3,0},{4,7},{5,6},{6,5},{7,4},{8,11},{9,10},{10,... | collective-permute-start | bytes 3145736 | tf_op jit(solution)/shard_map/ppermute | solution.py:23
  1085.2 204.9 %collective-permute-start.7 = (f32[2,32,4096]{2,1,0:T(8,128)}, f32[2,32,4096]{2,1,0:T(8,128)S(1)}, u32[]{:S(2)}, u32[]{:S(2)}) collective-permute-start(f32[2,32,4096]{2,1,0:T(8,128)} %get-tuple-element.13), channel_id=1, source_target_pairs={{0,4},{1,5},{2,6},{3,7},{4,0},{5,1},{6,2},{7,3},{8,12},{9,13},{10,... | collective-permute-start | bytes 3145736 | tf_op jit(solution)/shard_map/ppermute | solution.py:23
  1087.7 224.9 %collective-permute-start.8 = (f32[2,32,4096]{2,1,0:T(8,128)S(1)}, f32[2,32,4096]{2,1,0:T(8,128)S(1)}, u32[]{:S(2)}, u32[]{:S(2)}) collective-permute-start(f32[2,32,4096]{2,1,0:T(8,128)S(1)} %get-tuple-element.12), channel_id=1, source_target_pairs={{0,5},{1,4},{2,7},{3,6},{4,1},{5,0},{6,3},{7,2},{8,13},{9,12},{10,... | collective-permute-start | bytes 3145736 | tf_op jit(solution)/shard_map/ppermute | solution.py:23
  1087.9 249.6 %collective-permute-start.9 = (f32[2,32,4096]{2,1,0:T(8,128)S(1)}, f32[2,32,4096]{2,1,0:T(8,128)S(1)}, u32[]{:S(2)}, u32[]{:S(2)}) collective-permute-start(f32[2,32,4096]{2,1,0:T(8,128)S(1)} %get-tuple-element.11), channel_id=1, source_target_pairs={{0,6},{1,7},{2,4},{3,5},{4,2},{5,3},{6,0},{7,1},{8,14},{9,15},{10,... | collective-permute-start | bytes 3145736 | tf_op jit(solution)/shard_map/ppermute | solution.py:23
  1156.6 202.3 %collective-permute-start.10 = (f32[2,32,4096]{2,1,0:T(8,128)S(1)}, f32[2,32,4096]{2,1,0:T(8,128)S(1)}, u32[]{:S(2)}, u32[]{:S(2)}) collective-permute-start(f32[2,32,4096]{2,1,0:T(8,128)S(1)} %get-tuple-element.10), channel_id=1, source_target_pairs={{0,7},{1,6},{2,5},{3,4},{4,3},{5,2},{6,1},{7,0},{8,15},{9,14},{10,... | collective-permute-start | bytes 3145736 | tf_op jit(solution)/shard_map/ppermute | solution.py:23
  1545.2 99.0 %all-to-all-start.6 = ((f32[2,128,8192]{1,0,2:T(2,128)}), f32[2,128,8192]{1,0,2:T(2,128)}, u32[]{:S(2)}, u32[]{:S(2)}) async-start(f32[2,128,8192]{1,0,2:T(2,128)} %copy.166), calls=%async_computation.6 | async-start | bytes 16777216 | tf_op jit(solution)/shard_map/all_to_all | solution.py:177
  1644.2 97.9 %all-to-all-start.5 = ((f32[2,128,8192]{1,0,2:T(2,128)}), f32[2,128,8192]{1,0,2:T(2,128)}, u32[]{:S(2)}, u32[]{:S(2)}) async-start(f32[2,128,8192]{1,0,2:T(2,128)} %copy.161), calls=%async_computation.5 | async-start | bytes 16777216 | tf_op jit(solution)/shard_map/all_to_all | solution.py:176
  1749.8 25.5 %copy-start.1 = (f32[2,2,8]{2,1,0:T(2,128)S(1)}, f32[2,2,8]{2,1,0:T(2,128)}, u32[]{:S(2)}) copy-start(f32[2,2,8]{2,1,0:T(2,128)} %param.5) | copy-start | bytes 388
  (8 other events, 90.5 us)
